TPU v7x, 512 devices: a whole 4x8x8 slice. The times are simulated.
512 devices in a mesh: outer: 16 (over y, core), inner: 32 (over x, z).
Axes of the slice: x: 4, y: 8, z: 8, core: 2. Of those that a mesh axis runs over, the one named last changes fastest.
Arguments:
- queries: bfloat16 [32768, 4096], P('inner', 'outer'), may hold values from -150 to 150
- keys: bfloat16 [32768, 4096], P('inner', 'outer'), may hold values from -7 to 7
- values: bfloat16 [32768, 4096], P('inner', 'outer'), may hold values from -18 to 18
- counts: int32 [256], P('inner'), may hold values from 1 to 128, 24576 in all
- window_mask: int32 [256, 3], P('inner'), may hold values 0 or 1
- norm_gain: float32 [4096], P('outer'), may hold values from 0.5 to 1.5
Outputs:
- attended: bfloat16 [32768, 4096], P('inner', 'outer')
Inputs may be any that keep to these rules, and one draw needn't show every extreme that they name: `counts`: the largest count is exactly 128.
All inputs are finite; a program needn't handle non-finite values. No bound on the sum of `counts` or of `window_mask` on one device may be relied on, other than what follows from the above.
Results may differ from a plain program's by a relative error of at most 0.0048.
Values may be sent and summed in bfloat16 or wider, within the bound.
A program may use at most 64 MiB of HBM per device.

v0:
```python
import jax
import jax.numpy as jnp
from jax import lax
from jax.sharding import PartitionSpec as P

HD = 128
BLK = 128
PREV = 3
WIDTH = 4096


def carried_in(part, axis, combine, identity):
    place = lax.axis_index(axis)
    gathered = lax.all_gather(part, axis)
    state = jnp.zeros_like(part) + jnp.asarray(identity, part.dtype)

    def one(step, state):
        return combine(state, lax.dynamic_index_in_dim(gathered, step, 0, False))

    return lax.fori_loop(0, place, one, state)


def from_behind(value, axis, steps):
    count = lax.axis_size(axis)
    first, last = (max(0, -steps), min(count, count - steps))
    return lax.ppermute(value, axis, [(source, source + steps) for source in range(first, last)])


def add_states(earlier, later):
    return earlier + later


def shards(queries, keys, values, counts, window_mask, norm_gain):
    tok_rows = queries.shape[0]
    groups_here = tok_rows // BLK
    local_heads = queries.shape[1] // HD
    position = lax.broadcasted_iota(jnp.int32, (BLK,), 0)
    key_valid = position[None, :] < counts[:, None]
    masked_keys = jnp.where(key_valid.reshape(tok_rows)[:, None], keys, jnp.zeros((), jnp.bfloat16))
    query_blocks = queries.reshape(groups_here, BLK, local_heads, HD)
    key_blocks = masked_keys.reshape(groups_here, BLK, local_heads, HD)
    value_blocks = values.reshape(groups_here, BLK, local_heads, HD)
    group_states = jnp.einsum(
        "cshd,cshe->chde", key_blocks, value_blocks, preferred_element_type=jnp.float32
    )
    running = jnp.cumsum(group_states, axis=0)
    within = jnp.concatenate([jnp.zeros_like(group_states[:1]), running[:-1]], axis=0)
    span_total = running[-1]
    before = carried_in(span_total, "inner", add_states, jnp.zeros_like(span_total))
    prior_rounded = (before[None] + within).astype(jnp.bfloat16)
    rim_rows = PREV * BLK
    rim_keys, rim_values, rim_counts = from_behind(
        (
            masked_keys[tok_rows - rim_rows :],
            values[tok_rows - rim_rows :],
            counts[groups_here - PREV :],
        ),
        "inner",
        1,
    )
    extended_keys = jnp.concatenate([rim_keys, masked_keys], axis=0).reshape(
        groups_here + PREV, BLK, local_heads, HD
    )
    extended_values = jnp.concatenate([rim_values, values], axis=0).reshape(
        groups_here + PREV, BLK, local_heads, HD
    )
    extended_counts = jnp.concatenate([rim_counts, counts], axis=0)
    extended_valid = position[None, :] < extended_counts[:, None]
    window_keys = jnp.stack(
        [extended_keys[place : place + groups_here] for place in range(PREV + 1)], axis=1
    ).reshape(groups_here, (PREV + 1) * BLK, local_heads, HD)
    window_values = jnp.stack(
        [extended_values[place : place + groups_here] for place in range(PREV + 1)], axis=1
    ).reshape(groups_here, (PREV + 1) * BLK, local_heads, HD)
    window_valid = jnp.stack(
        [extended_valid[place : place + groups_here] for place in range(PREV + 1)], axis=1
    )
    group_on = jnp.concatenate(
        [window_mask[:, ::-1] == 1, jnp.ones((groups_here, 1), jnp.bool_)], axis=1
    )
    causal = position[:, None] >= position[None, :]
    causal_full = jnp.concatenate([jnp.ones((BLK, PREV * BLK), jnp.bool_), causal], axis=1)
    allowed = (window_valid & group_on[:, :, None]).reshape(
        groups_here, 1, (PREV + 1) * BLK
    ) & causal_full[None]
    score_scale = 1.0 / HD**0.5
    scores = (
        jnp.einsum("cthd,cshd->chts", query_blocks, window_keys, preferred_element_type=jnp.float32)
        * score_scale
    )
    scores = jnp.where(allowed[:, None], scores, -1e30)
    largest = jnp.max(scores, axis=-1, keepdims=True)
    expd = jnp.exp(scores - largest)
    weights = (expd / jnp.sum(expd, axis=-1, keepdims=True)).astype(jnp.bfloat16)
    local_part = jnp.einsum(
        "chts,cshd->cthd", weights, window_values, preferred_element_type=jnp.float32
    )
    inter = jnp.einsum(
        "cthd,chde->cthe", query_blocks, prior_rounded, preferred_element_type=jnp.float32
    )
    intra_weights = jnp.einsum(
        "cthd,cshd->chts", query_blocks, key_blocks, preferred_element_type=jnp.float32
    )
    intra_weights = jnp.where(causal[None, None], intra_weights, 0.0).astype(jnp.bfloat16)
    intra = jnp.einsum(
        "chts,cshe->cthe", intra_weights, value_blocks, preferred_element_type=jnp.float32
    )
    linear_part = inter + intra
    local_squares = jnp.sum(linear_part * linear_part, axis=(2, 3))
    row_squares = lax.psum(local_squares, "outer")
    normed = linear_part * lax.rsqrt(row_squares / WIDTH + 1e-06)[:, :, None, None]
    result = normed * norm_gain.reshape(local_heads, HD)[None, None] + local_part
    return result.reshape(tok_rows, local_heads * HD).astype(jnp.bfloat16)


def solution(mesh):
    return jax.shard_map(
        shards,
        mesh=mesh,
        in_specs=(
            P("inner", "outer"),
            P("inner", "outer"),
            P("inner", "outer"),
            P("inner"),
            P("inner", None),
            P("outer"),
        ),
        out_specs=P("inner", "outer"),
        check_vma=False,
    )
```

profile of v0, /device:TPU:7, one launch (start us, length us, event | category | flops | bytes accessed | tf_op | source)
XLA Modules:
  0.0 166.0 jit_solution(16054141134522092386)
XLA Ops:
  7.3 1.2 broadcast_select_fusion
  8.7 1.2 reshape.85
  13.4 4.0 %collective-permute-start.2 = (bf16[384,256]{1,0:T(8,128)(2,1)}, bf16[384,256]{1,0:T(8,128)(2,1)S(1)}, u32[]{:S(2)}, u32[]{:S(2)}) collective-permute-start(bf16[384,256]{1,0:T(8,128)(2,1)} %slice.79), channel_id=1, source_target_pairs={{0,1},{1,2},{2,3},{3,4},{4,5},{5,6},{6,7},{7,8},{8,9},{9,10},{10,1... | collective-permute-start | bytes 589832 | tf_op jit(solution)/shard_map/ppermute | solution.py:26
  18.1 4.0 %collective-permute-start.1 = (s32[3]{0:T(128)}, s32[3]{0:T(128)}, u32[]{:S(2)}, u32[]{:S(2)}) collective-permute-start(s32[3]{0:T(128)} %slice.61), channel_id=1, source_target_pairs={{0,1},{1,2},{2,3},{3,4},{4,5},{5,6},{6,7},{7,8},{8,9},{9,10},{10,1... | collective-permute-start | bytes 44 | tf_op jit(solution)/shard_map/ppermute | solution.py:26
  22.8 4.0 %collective-permute-start = (bf16[384,256]{1,0:T(8,128)(2,1)}, bf16[384,256]{1,0:T(8,128)(2,1)S(1)}, u32[]{:S(2)}, u32[]{:S(2)}) collective-permute-start(bf16[384,256]{1,0:T(8,128)(2,1)} %slice.57), channel_id=1, source_target_pairs={{0,1},{1,2},{2,3},{3,4},{4,5},{5,6},{6,7},{7,8},{8,9},{9,10},{10,1... | collective-permute-start | bytes 589832 | tf_op jit(solution)/shard_map/ppermute | solution.py:26
  28.6 2.0 %copy.56 = bf16[8,1,128,2,128]{4,2,1,3,0:T(8,128)(2,1)} copy(bf16[8,1,128,2,128]{4,3,2,0,1:T(2,128)(2,1)} %stack.58) | data formatting | bytes 1048576 | tf_op jit(solution)/shard_map/stack | solution.py:69
  30.6 1.2 reshape.86
  31.9 3.8 %copy.52 = bf16[8,1,128,2,128]{2,1,4,3,0:T(2,128)(2,1)} copy(bf16[8,1,128,2,128]{4,3,2,0,1:T(2,128)(2,1)} %stack.48) | data formatting | bytes 1048576 | tf_op jit(solution)/shard_map/stack | solution.py:72
  36.6 1.4 broadcast_and_fusion
  38.9 1.2 stack.55
  44.2 1.2 stack.45
  45.4 2.0 %copy.49 = bf16[8,1,128,2,128]{2,1,4,3,0:T(2,128)(2,1)} copy(bf16[8,1,128,2,128]{4,3,2,0,1:T(2,128)(2,1)S(1)} %stack.45) | data formatting | bytes 1048576 | tf_op jit(solution)/shard_map/stack | solution.py:72
  48.6 2.0 %copy.50 = bf16[8,1,128,2,128]{2,1,4,3,0:T(2,128)(2,1)} copy(bf16[8,1,128,2,128]{4,3,2,0,1:T(2,128)(2,1)S(1)} %stack.46) | data formatting | bytes 1048576 | tf_op jit(solution)/shard_map/stack | solution.py:72
  50.7 2.0 %copy.51 = bf16[8,1,128,2,128]{2,1,4,3,0:T(2,128)(2,1)} copy(bf16[8,1,128,2,128]{4,3,2,0,1:T(2,128)(2,1)S(1)} %stack.47) | data formatting | bytes 1048576 | tf_op jit(solution)/shard_map/stack | solution.py:72
  52.7 6.4 %pad_maximum_fusion = bf16[8,4,128,2,128]{2,1,4,3,0:T(4,128)(2,1)S(1)} fusion(bf16[8,1,128,2,128]{2,1,4,3,0:T(2,128)(2,1)} %copy.52, bf16[8,1,128,2,128]{2,1,4,3,0:T(2,128)(2,1)} %copy.51, bf16[8,1,128,2,128]{2,1,4,3,0:T(2,128)(2,1)} %copy.50, bf16[8,1,128,2,128]{2,1,4,3,0:T(2,128)(2,1)} %copy.49), kind=kLoop, calls=%fused_computation.6 | loop fusion | flops 8388608 | bytes 4194304 | tf_op jit(solution)/shard_map/stack | solution.py:72
  59.1 2.2 %reshape.87 = bf16[8,512,2,128]{1,3,2,0:T(8,128)(2,1)} reshape(bf16[8,4,128,2,128]{2,1,4,3,0:T(4,128)(2,1)S(1)} %pad_maximum_fusion) | data formatting | bytes 4194304 | tf_op jit(solution)/shard_map/reshape | solution.py:74
  61.3 1.8 %pad_maximum_fusion.1 = bf16[8,4,128,2,128]{4,2,1,3,0:T(8,128)(2,1)S(1)} fusion(bf16[8,1,128,2,128]{4,2,1,3,0:T(8,128)(2,1)} %copy.56, bf16[8,1,128,2,128]{4,2,1,3,0:T(8,128)(2,1)} %copy.55, bf16[8,1,128,2,128]{4,2,1,3,0:T(8,128)(2,1)} %copy.54, bf16[8,1,128,2,128]{4,2,1,3,0:T(8,128)(2,1)} %copy.53), kind=kLoop, calls=%fused_computation.7 | loop fusion | flops 3145728 | bytes 4194304 | tf_op jit(solution)/shard_map/stack | solution.py:69
  64.2 3.9 %fusion.33 = (f32[8,2,128]{2,1,0:T(2,128)S(1)}, f32[8,2,128,512]{2,3,1,0:T(8,128)}) fusion(f32[8,2,512,128]{3,2,1,0:T(8,128)S(1)} %fusion.21, pred[8,128,512]{1,2,0:T(8,128)(4,1)S(1)} %copy-done.4), kind=kOutput, calls=%fused_computation.63 | output fusion | flops 6291967 | bytes 8921088 | tf_op jit(solution)/shard_map/sub | solution.py:93
  68.0 32.9 %all-gather.2.cloned.1.call-done = f32[32,2,128,128]{3,2,1,0:T(8,128)} async-done(((f32[1,2,128,128]{3,2,1,0:T(8,128)}), f32[32,2,128,128]{3,2,1,0:T(8,128)}) %all-gather.2.cloned.1.call-update) | async-done | bytes 4194320 | tf_op jit(solution)/shard_map/all_gather | solution.py:14
  100.9 23.1 %while.10 = (s32[]{:T(128)}, f32[2,128,128]{2,1,0:T(8,128)S(1)}, s32[]{:T(128)}, f32[32,2,128,128]{3,2,1,0:T(8,128)}, s32[]{:T(128)}, /*index=5*/s32[]{:T(128)}, s32[]{:T(128)}) while((s32[]{:T(128)}, f32[2,128,128]{2,1,0:T(8,128)S(1)}, s32[]{:T(128)}, f32[32,2,128,128]{3,2,1,0:T(8,128)}, s32[]{:T(128)}, /*index=5*/s32[]{:T(128)}, ...), condition=%wide.region_2.3_spmd, body=%wide.region_1.2_spmd.sunk | while | flops 32773 | bytes 393331 | solution.py:20
  124.1 1.5 convolution_bitcast_fusion.2
  125.6 1.9 %multiply_reduce_fusion = (f32[8,128]{1,0:T(8,128)S(1)}, f32[8,128,2,128]{1,3,2,0:T(8,128)S(1)}) fusion(f32[8,128,2,128]{1,3,2,0:T(8,128)} %convolution_bitcast_fusion.2, bf16[8,128,2,128]{1,3,2,0:T(8,128)(2,1)S(1)} %copy-done.2, pred[128,128]{0,1:T(8,128)(4,1)S(1)} %iota_compare_fusion, bf16[8,128,2,128]{3,2,1,0:T(2,128)(2,1)S(1)} %reshape.84, ...), kind=kOutput, calls=%fused_computation.21 | convolution fusion | flops 135527424 | bytes 3690496 | tf_op jit(solution)/shard_map/chts,cshe->cthe/dot_general | solution.py:105
  127.5 26.7 %psum.7 = f32[8,128]{1,0:T(8,128)S(1)} all-reduce(f32[8,128]{1,0:T(8,128)S(1)} %get-tuple-element.49), channel_id=1, replica_groups=mesh['outer'=16,'inner'=32] {'outer'}, use_global_device_ids=true, to_apply=%region_4.5 | all-reduce | flops 1024 | bytes 8192 | tf_op jit(solution)/shard_map/psum | solution.py:110
  154.2 3.5 %fusion.10 = bf16[8,128,2,128]{1,3,2,0:T(8,128)(2,1)S(1)} fusion(bf16[8,512,2,128]{1,3,2,0:T(8,128)(2,1)} %reshape.87, f32[8,2,128,512]{2,3,1,0:T(8,128)} %get-tuple-element.48, f32[8,2,128]{2,1,0:T(2,128)S(1)} %get-tuple-element.47, f32[8,128,2,128]{1,3,2,0:T(8,128)S(1)} %get-tuple-element.50, f32[2,128]{1,0:T(2,128)S(1)} %bitcast.65, ...), kind=kOutput, calls=%fused_computation.19 | convolution fusion | flops 271581184 | bytes 7877632 | tf_op jit(solution)/shard_map/chts,cshd->cthd/dot_general | solution.py:95
  (83 shorter events, 39.7 us)
Async XLA Ops:
  6.5 94.4 %all-gather.2.cloned.1.call-start = ((), (), s32[]{:S(2)}) async-start(), calls=%async_computation | async-start | bytes 4325376 | tf_op jit(solution)/shard_map/all_gather | solution.py:14
  8.5 8.9 %copy-start.7 = (s32[8]{0:T(128)S(1)}, s32[8]{0:T(128)}, u32[]{:S(2)}) copy-start(s32[8]{0:T(128)} %param.11) | copy-start | bytes 100
  8.5 13.5 %copy-start = (bf16[1024,256]{1,0:T(8,128)(2,1)S(1)}, bf16[1024,256]{1,0:T(8,128)(2,1)}, u32[]{:S(2)}) copy-start(bf16[1024,256]{1,0:T(8,128)(2,1)} %param.10) | copy-start | bytes 1572868
  10.3 18.3 %copy-start.1 = (bf16[8,128,2,128]{1,3,2,0:T(8,128)(2,1)}, bf16[8,128,2,128]{1,3,2,0:T(8,128)(2,1)S(1)}, u32[]{:S(2)}) copy-start(bf16[8,128,2,128]{1,3,2,0:T(8,128)(2,1)S(1)} %copy.48) | copy-start | bytes 1572868
  10.8 20.9 %copy-start.5 = (s32[8,3]{0,1:T(4,128)S(1)}, s32[8,3]{0,1:T(4,128)}, u32[]{:S(2)}) copy-start(s32[8,3]{0,1:T(4,128)} %param.12) | copy-start | bytes 292
  11.9 16.6 %copy-start.3 = (f32[8,2,128,128]{3,2,1,0:T(8,128)}, f32[8,2,128,128]{3,2,1,0:T(8,128)S(1)}, u32[]{:S(2)}) copy-start(f32[8,2,128,128]{3,2,1,0:T(8,128)S(1)} %fusion.38) | copy-start | bytes 3145732
  13.4 24.6 %collective-permute-start.2 = (bf16[384,256]{1,0:T(8,128)(2,1)}, bf16[384,256]{1,0:T(8,128)(2,1)S(1)}, u32[]{:S(2)}, u32[]{:S(2)}) collective-permute-start(bf16[384,256]{1,0:T(8,128)(2,1)} %slice.79), channel_id=1, source_target_pairs={{0,1},{1,2},{2,3},{3,4},{4,5},{5,6},{6,7},{7,8},{8,9},{9,10},{10,1... | collective-permute-start | bytes 589832 | tf_op jit(solution)/shard_map/ppermute | solution.py:26
  18.1 17.6 %collective-permute-start.1 = (s32[3]{0:T(128)}, s32[3]{0:T(128)}, u32[]{:S(2)}, u32[]{:S(2)}) collective-permute-start(s32[3]{0:T(128)} %slice.61), channel_id=1, source_target_pairs={{0,1},{1,2},{2,3},{3,4},{4,5},{5,6},{6,7},{7,8},{8,9},{9,10},{10,1... | collective-permute-start | bytes 44 | tf_op jit(solution)/shard_map/ppermute | solution.py:26
  22.8 20.3 %collective-permute-start = (bf16[384,256]{1,0:T(8,128)(2,1)}, bf16[384,256]{1,0:T(8,128)(2,1)S(1)}, u32[]{:S(2)}, u32[]{:S(2)}) collective-permute-start(bf16[384,256]{1,0:T(8,128)(2,1)} %slice.57), channel_id=1, source_target_pairs={{0,1},{1,2},{2,3},{3,4},{4,5},{5,6},{6,7},{7,8},{8,9},{9,10},{10,1... | collective-permute-start | bytes 589832 | tf_op jit(solution)/shard_map/ppermute | solution.py:26
  63.1 1.0 copy-start.4
  64.2 59.9 %slice-start = ((f32[8,2,128,128]{3,2,1,0:T(8,128)}), f32[7,2,128,128]{3,2,1,0:T(8,128)S(1)}, s32[]{:S(2)}) async-start(f32[8,2,128,128]{3,2,1,0:T(8,128)} %copy-done.3), calls=%async_computation.1 | async-start | bytes 1835008 | tf_op jit(solution)/shard_map/slice | solution.py:47
  68.0 57.6 %copy-start.2 = (bf16[8,128,2,128]{1,3,2,0:T(8,128)(2,1)S(1)}, bf16[8,128,2,128]{1,3,2,0:T(8,128)(2,1)}, u32[]{:S(2)}) copy-start(bf16[8,128,2,128]{1,3,2,0:T(8,128)(2,1)} %copy-done.1) | copy-start | bytes 1572868
  100.9 53.3 %copy-start.6 = (f32[256]{0:T(256)S(1)}, f32[256]{0:T(256)}, u32[]{:S(2)}) copy-start(f32[256]{0:T(256)} %param.13) | copy-start | bytes 3076
Sparse Core Ops, SparseCore 0:
  12.8 88.0 all-gather.1
where the time goes:
time: 167 us; the launch traced here: 166 us
  other arithmetic  40.8 us (24%)
  waiting for transfers between devices  32.9 us (20%)
  local copies, waits for them, and re-layouts  31 us (19%)
  blocking collectives  26.7 us (16%)
  between operations  13.6 us (8%)
  starting transfers between devices  12 us (7%)
  matrix products  8.16 us (5%)
    all_gather x1, waiting for transfers between devices, carried_in(): gathered = lax.all_gather(part, axis)  32.9 us
    psum x1, blocking collectives, shards(): row_squares = lax.psum(local_squares, 'outer')  26.7 us
    add x24, other arithmetic, add_states(): return earlier + later  22.5 us
    another operation x8, local copies, waits for them, and re-layouts, shards(): jnp.stack([extended_values[place:place + groups_here] for place in range(...  13.2 us
    ppermute x3, starting transfers between devices, from_behind(): lax.ppermute(value, axis, [(source, source + steps) for source in range(f...  12 us
    another operation x8, local copies, waits for them, and re-layouts, shards(): jnp.stack([extended_keys[place:place + groups_here] for place in range(PR...  7.08 us
    another operation x1, other arithmetic, shards(): jnp.stack([extended_values[place:place + groups_here] for place in range(...  6.43 us
    sub x1, other arithmetic, shards(): expd = jnp.exp(scores - largest)  3.88 us
  transfers between devices with their start and end apart: 4, of which 1 were waited for; matrix products, arithmetic and copies ran while one was open for 26% of the time, Pallas kernels for 0%

commit v1 on v0

--- a/solution.py
+++ b/solution.py
@@ -107,7 +107,7 @@
     )
     linear_part = inter + intra
     local_squares = jnp.sum(linear_part * linear_part, axis=(2, 3))
-    row_squares = lax.psum(local_squares, "outer")
+    row_squares = jnp.sum(lax.all_gather(local_squares, "outer"), axis=0)
     normed = linear_part * lax.rsqrt(row_squares / WIDTH + 1e-06)[:, :, None, None]
     result = normed * norm_gain.reshape(local_heads, HD)[None, None] + local_part
     return result.reshape(tok_rows, local_heads * HD).astype(jnp.bfloat16)

time: 167 us -> 161 us (0.964)
  blocking collectives: 26.7 us -> 20.8 us
    psum x1 -> x0, blocking collectives: 26.7 us -> none  [shards(): row_squares = lax.psum(local_squares, 'outer')]
    all_gather x0 -> x1, blocking collectives: none -> 20.8 us  [shards(): row_squares = jnp.sum(lax.all_gather(local_squares, 'outer'), axis=0)]
  transfers between devices with their start and end apart: 4 -> 4, of which waited for: 1 -> 1; matrix products, arithmetic and copies ran while one was open for 26% -> 27% of each run, Pallas kernels for 0% -> 0%
where the time goes in v1:
time: 161 us; the launch traced here: 160 us
  other arithmetic  40.9 us (25%)
  waiting for transfers between devices  32.9 us (20%)
  local copies, waits for them, and re-layouts  31 us (19%)
  blocking collectives  20.8 us (13%)
  between operations  13.7 us (9%)
  starting transfers between devices  12 us (7%)
  matrix products  8.16 us (5%)
    all_gather x1, waiting for transfers between devices, carried_in(): gathered = lax.all_gather(part, axis)  32.9 us
    add x24, other arithmetic, add_states(): return earlier + later  22.5 us
    all_gather x1, blocking collectives, shards(): row_squares = jnp.sum(lax.all_gather(local_squares, 'outer'), axis=0)  20.8 us
    another operation x8, local copies, waits for them, and re-layouts, shards(): jnp.stack([extended_values[place:place + groups_here] for place in range(...  13.2 us
    ppermute x3, starting transfers between devices, from_behind(): lax.ppermute(value, axis, [(source, source + steps) for source in range(f...  12 us
    another operation x8, local copies, waits for them, and re-layouts, shards(): jnp.stack([extended_keys[place:place + groups_here] for place in range(PR...  7.08 us
    another operation x1, other arithmetic, shards(): jnp.stack([extended_values[place:place + groups_here] for place in range(...  6.43 us
    sub x1, other arithmetic, shards(): expd = jnp.exp(scores - largest)  3.88 us
  transfers between devices with their start and end apart: 4, of which 1 were waited for; matrix products, arithmetic and copies ran while one was open for 27% of the time, Pallas kernels for 0%

profile of v1, /device:TPU:7, one launch (start us, length us, event | category | flops | bytes accessed | tf_op | source)
XLA Modules:
  0.0 160.0 jit_solution(15511953102851819945)
XLA Ops:
  7.3 1.2 broadcast_select_fusion
  8.7 1.2 reshape.89
  13.4 4.0 %collective-permute-start.2 = (bf16[384,256]{1,0:T(8,128)(2,1)}, bf16[384,256]{1,0:T(8,128)(2,1)S(1)}, u32[]{:S(2)}, u32[]{:S(2)}) collective-permute-start(bf16[384,256]{1,0:T(8,128)(2,1)} %slice.79), channel_id=1, source_target_pairs={{0,1},{1,2},{2,3},{3,4},{4,5},{5,6},{6,7},{7,8},{8,9},{9,10},{10,1... | collective-permute-start | bytes 589832 | tf_op jit(solution)/shard_map/ppermute | solution.py:26
  18.1 4.0 %collective-permute-start.1 = (s32[3]{0:T(128)}, s32[3]{0:T(128)}, u32[]{:S(2)}, u32[]{:S(2)}) collective-permute-start(s32[3]{0:T(128)} %slice.61), channel_id=1, source_target_pairs={{0,1},{1,2},{2,3},{3,4},{4,5},{5,6},{6,7},{7,8},{8,9},{9,10},{10,1... | collective-permute-start | bytes 44 | tf_op jit(solution)/shard_map/ppermute | solution.py:26
  22.8 4.0 %collective-permute-start = (bf16[384,256]{1,0:T(8,128)(2,1)}, bf16[384,256]{1,0:T(8,128)(2,1)S(1)}, u32[]{:S(2)}, u32[]{:S(2)}) collective-permute-start(bf16[384,256]{1,0:T(8,128)(2,1)} %slice.57), channel_id=1, source_target_pairs={{0,1},{1,2},{2,3},{3,4},{4,5},{5,6},{6,7},{7,8},{8,9},{9,10},{10,1... | collective-permute-start | bytes 589832 | tf_op jit(solution)/shard_map/ppermute | solution.py:26
  28.6 2.0 %copy.76 = bf16[8,1,128,2,128]{4,2,1,3,0:T(8,128)(2,1)} copy(bf16[8,1,128,2,128]{4,3,2,0,1:T(2,128)(2,1)} %stack.58) | data formatting | bytes 1048576 | tf_op jit(solution)/shard_map/stack | solution.py:69
  30.6 1.2 reshape.90
  31.9 3.8 %copy.72 = bf16[8,1,128,2,128]{2,1,4,3,0:T(2,128)(2,1)} copy(bf16[8,1,128,2,128]{4,3,2,0,1:T(2,128)(2,1)} %stack.48) | data formatting | bytes 1048576 | tf_op jit(solution)/shard_map/stack | solution.py:72
  36.6 1.4 broadcast_and_fusion
  38.9 1.2 stack.55
  44.2 1.2 stack.45
  45.4 2.0 %copy.69 = bf16[8,1,128,2,128]{2,1,4,3,0:T(2,128)(2,1)} copy(bf16[8,1,128,2,128]{4,3,2,0,1:T(2,128)(2,1)S(1)} %stack.45) | data formatting | bytes 1048576 | tf_op jit(solution)/shard_map/stack | solution.py:72
  48.6 2.0 %copy.70 = bf16[8,1,128,2,128]{2,1,4,3,0:T(2,128)(2,1)} copy(bf16[8,1,128,2,128]{4,3,2,0,1:T(2,128)(2,1)S(1)} %stack.46) | data formatting | bytes 1048576 | tf_op jit(solution)/shard_map/stack | solution.py:72
  50.7 2.0 %copy.71 = bf16[8,1,128,2,128]{2,1,4,3,0:T(2,128)(2,1)} copy(bf16[8,1,128,2,128]{4,3,2,0,1:T(2,128)(2,1)S(1)} %stack.47) | data formatting | bytes 1048576 | tf_op jit(solution)/shard_map/stack | solution.py:72
  52.7 6.4 %pad_maximum_fusion = bf16[8,4,128,2,128]{2,1,4,3,0:T(4,128)(2,1)S(1)} fusion(bf16[8,1,128,2,128]{2,1,4,3,0:T(2,128)(2,1)} %copy.72, bf16[8,1,128,2,128]{2,1,4,3,0:T(2,128)(2,1)} %copy.71, bf16[8,1,128,2,128]{2,1,4,3,0:T(2,128)(2,1)} %copy.70, bf16[8,1,128,2,128]{2,1,4,3,0:T(2,128)(2,1)} %copy.69), kind=kLoop, calls=%fused_computation.6 | loop fusion | flops 8388608 | bytes 4194304 | tf_op jit(solution)/shard_map/stack | solution.py:72
  59.1 2.2 %reshape.91 = bf16[8,512,2,128]{1,3,2,0:T(8,128)(2,1)} reshape(bf16[8,4,128,2,128]{2,1,4,3,0:T(4,128)(2,1)S(1)} %pad_maximum_fusion) | data formatting | bytes 4194304 | tf_op jit(solution)/shard_map/reshape | solution.py:74
  61.3 1.8 %pad_maximum_fusion.1 = bf16[8,4,128,2,128]{4,2,1,3,0:T(8,128)(2,1)S(1)} fusion(bf16[8,1,128,2,128]{4,2,1,3,0:T(8,128)(2,1)} %copy.76, bf16[8,1,128,2,128]{4,2,1,3,0:T(8,128)(2,1)} %copy.75, bf16[8,1,128,2,128]{4,2,1,3,0:T(8,128)(2,1)} %copy.74, bf16[8,1,128,2,128]{4,2,1,3,0:T(8,128)(2,1)} %copy.73), kind=kLoop, calls=%fused_computation.7 | loop fusion | flops 3145728 | bytes 4194304 | tf_op jit(solution)/shard_map/stack | solution.py:69
  64.2 3.9 %fusion.33 = (f32[8,2,128]{2,1,0:T(2,128)S(1)}, f32[8,2,128,512]{2,3,1,0:T(8,128)}) fusion(f32[8,2,512,128]{3,2,1,0:T(8,128)S(1)} %fusion.21, pred[8,128,512]{1,2,0:T(8,128)(4,1)S(1)} %copy-done.4), kind=kOutput, calls=%fused_computation.64 | output fusion | flops 6291967 | bytes 8921088 | tf_op jit(solution)/shard_map/sub | solution.py:93
  68.0 32.9 %all-gather.3.cloned.1.call-done = f32[32,2,128,128]{3,2,1,0:T(8,128)} async-done(((f32[1,2,128,128]{3,2,1,0:T(8,128)}), f32[32,2,128,128]{3,2,1,0:T(8,128)}) %all-gather.3.cloned.1.call-update) | async-done | bytes 4194320 | tf_op jit(solution)/shard_map/all_gather | solution.py:14
  100.9 23.1 %while.10 = (s32[]{:T(128)}, f32[2,128,128]{2,1,0:T(8,128)S(1)}, s32[]{:T(128)}, f32[32,2,128,128]{3,2,1,0:T(8,128)}, s32[]{:T(128)}, /*index=5*/s32[]{:T(128)}, s32[]{:T(128)}) while((s32[]{:T(128)}, f32[2,128,128]{2,1,0:T(8,128)S(1)}, s32[]{:T(128)}, f32[32,2,128,128]{3,2,1,0:T(8,128)}, s32[]{:T(128)}, /*index=5*/s32[]{:T(128)}, ...), condition=%wide.region_2.3_spmd, body=%wide.region_1.2_spmd.sunk | while | flops 32773 | bytes 393331 | solution.py:20
  124.1 1.5 convolution_bitcast_fusion.2
  125.6 1.9 %multiply_reduce_fusion = (f32[8,128]{1,0:T(8,128)S(1)}, f32[8,128,2,128]{1,3,2,0:T(8,128)S(1)}) fusion(f32[8,128,2,128]{1,3,2,0:T(8,128)} %convolution_bitcast_fusion.2, bf16[8,128,2,128]{1,3,2,0:T(8,128)(2,1)S(1)} %copy-done.2, pred[128,128]{0,1:T(8,128)(4,1)S(1)} %iota_compare_fusion, bf16[8,128,2,128]{3,2,1,0:T(2,128)(2,1)S(1)} %reshape.88, ...), kind=kOutput, calls=%fused_computation.21 | convolution fusion | flops 135527424 | bytes 3690496 | tf_op jit(solution)/shard_map/chts,cshe->cthe/dot_general | solution.py:105
  127.5 20.8 %all-gather = f32[128,128]{1,0:T(8,128)S(1)} all-gather(f32[8,128]{1,0:T(8,128)S(1)} %get-tuple-element.49), channel_id=2, replica_groups=mesh['outer'=16,'inner'=32] {'outer'}, dimensions={0}, use_global_device_ids=true | all-gather | bytes 69632 | tf_op jit(solution)/shard_map/all_gather | solution.py:110
  148.3 3.5 %fusion.10 = bf16[8,128,2,128]{1,3,2,0:T(8,128)(2,1)S(1)} fusion(bf16[8,512,2,128]{1,3,2,0:T(8,128)(2,1)} %reshape.91, f32[8,2,128,512]{2,3,1,0:T(8,128)} %get-tuple-element.48, f32[8,2,128]{2,1,0:T(2,128)S(1)} %get-tuple-element.47, f32[8,128,2,128]{1,3,2,0:T(8,128)S(1)} %get-tuple-element.50, f32[2,128]{1,0:T(2,128)S(1)} %bitcast.67, ...), kind=kOutput, calls=%fused_computation.19 | convolution fusion | flops 271581184 | bytes 7877632 | tf_op jit(solution)/shard_map/chts,cshd->cthd/dot_general | solution.py:95
  (84 shorter events, 39.7 us)
Async XLA Ops:
  6.5 94.4 %all-gather.3.cloned.1.call-start = ((), (), s32[]{:S(2)}) async-start(), calls=%async_computation | async-start | bytes 4325376 | tf_op jit(solution)/shard_map/all_gather | solution.py:14
  8.5 8.9 %copy-start.7 = (s32[8]{0:T(128)S(1)}, s32[8]{0:T(128)}, u32[]{:S(2)}) copy-start(s32[8]{0:T(128)} %param.11) | copy-start | bytes 100
  8.5 13.5 %copy-start = (bf16[1024,256]{1,0:T(8,128)(2,1)S(1)}, bf16[1024,256]{1,0:T(8,128)(2,1)}, u32[]{:S(2)}) copy-start(bf16[1024,256]{1,0:T(8,128)(2,1)} %param.10) | copy-start | bytes 1572868
  10.3 18.3 %copy-start.1 = (bf16[8,128,2,128]{1,3,2,0:T(8,128)(2,1)}, bf16[8,128,2,128]{1,3,2,0:T(8,128)(2,1)S(1)}, u32[]{:S(2)}) copy-start(bf16[8,128,2,128]{1,3,2,0:T(8,128)(2,1)S(1)} %copy.68) | copy-start | bytes 1572868
  10.8 20.9 %copy-start.5 = (s32[8,3]{0,1:T(4,128)S(1)}, s32[8,3]{0,1:T(4,128)}, u32[]{:S(2)}) copy-start(s32[8,3]{0,1:T(4,128)} %param.12) | copy-start | bytes 292
  11.9 16.6 %copy-start.3 = (f32[8,2,128,128]{3,2,1,0:T(8,128)}, f32[8,2,128,128]{3,2,1,0:T(8,128)S(1)}, u32[]{:S(2)}) copy-start(f32[8,2,128,128]{3,2,1,0:T(8,128)S(1)} %fusion.38) | copy-start | bytes 3145732
  13.4 24.6 %collective-permute-start.2 = (bf16[384,256]{1,0:T(8,128)(2,1)}, bf16[384,256]{1,0:T(8,128)(2,1)S(1)}, u32[]{:S(2)}, u32[]{:S(2)}) collective-permute-start(bf16[384,256]{1,0:T(8,128)(2,1)} %slice.79), channel_id=1, source_target_pairs={{0,1},{1,2},{2,3},{3,4},{4,5},{5,6},{6,7},{7,8},{8,9},{9,10},{10,1... | collective-permute-start | bytes 589832 | tf_op jit(solution)/shard_map/ppermute | solution.py:26
  18.1 17.6 %collective-permute-start.1 = (s32[3]{0:T(128)}, s32[3]{0:T(128)}, u32[]{:S(2)}, u32[]{:S(2)}) collective-permute-start(s32[3]{0:T(128)} %slice.61), channel_id=1, source_target_pairs={{0,1},{1,2},{2,3},{3,4},{4,5},{5,6},{6,7},{7,8},{8,9},{9,10},{10,1... | collective-permute-start | bytes 44 | tf_op jit(solution)/shard_map/ppermute | solution.py:26
  22.8 20.3 %collective-permute-start = (bf16[384,256]{1,0:T(8,128)(2,1)}, bf16[384,256]{1,0:T(8,128)(2,1)S(1)}, u32[]{:S(2)}, u32[]{:S(2)}) collective-permute-start(bf16[384,256]{1,0:T(8,128)(2,1)} %slice.57), channel_id=1, source_target_pairs={{0,1},{1,2},{2,3},{3,4},{4,5},{5,6},{6,7},{7,8},{8,9},{9,10},{10,1... | collective-permute-start | bytes 589832 | tf_op jit(solution)/shard_map/ppermute | solution.py:26
  63.1 1.0 copy-start.4
  64.2 59.9 %slice-start = ((f32[8,2,128,128]{3,2,1,0:T(8,128)}), f32[7,2,128,128]{3,2,1,0:T(8,128)S(1)}, s32[]{:S(2)}) async-start(f32[8,2,128,128]{3,2,1,0:T(8,128)} %copy-done.3), calls=%async_computation.1 | async-start | bytes 1835008 | tf_op jit(solution)/shard_map/slice | solution.py:47
  68.0 57.6 %copy-start.2 = (bf16[8,128,2,128]{1,3,2,0:T(8,128)(2,1)S(1)}, bf16[8,128,2,128]{1,3,2,0:T(8,128)(2,1)}, u32[]{:S(2)}) copy-start(bf16[8,128,2,128]{1,3,2,0:T(8,128)(2,1)} %copy-done.1) | copy-start | bytes 1572868
  100.9 47.4 %copy-start.6 = (f32[256]{0:T(256)S(1)}, f32[256]{0:T(256)}, u32[]{:S(2)}) copy-start(f32[256]{0:T(256)} %param.13) | copy-start | bytes 3076
Sparse Core Ops, SparseCore 0:
  12.8 88.0 all-gather.2
